TPU v7x, 32 devices: a whole 2x2x4 slice. The times are simulated.
32 devices in a mesh: seq: 8 (over z, y), head: 4 (over x, core).
Axes of the slice: x: 2, y: 2, z: 4, core: 2. Of those that a mesh axis runs over, the one named last changes fastest.
Arguments:
- query: bfloat16 [4096, 8192], P('seq', 'head'), may hold values from -1.5 to 1.5
- key_in: bfloat16 [4096, 8192], P('seq', 'head'), may hold values from -0.5 to 0.5
- value: bfloat16 [4096, 8192], P('seq', 'head'), may hold values from -6 to 6
- gate: bfloat16 [4096, 8192], P(('seq', 'head')), may hold values from -6 to 6
- gain: float32 [8192], replicated, may hold values from 0.5 to 1.5
- grad_out: bfloat16 [4096, 8192], P(('seq', 'head')), may hold values from -6 to 6
Outputs:
- grad_query: bfloat16 [4096, 8192], P('seq', 'head')
- grad_key: bfloat16 [4096, 8192], P('seq', 'head')
- grad_value: bfloat16 [4096, 8192], P('seq', 'head')
- grad_gate: bfloat16 [4096, 8192], P(('seq', 'head'))
All inputs are finite; a program needn't handle non-finite values.
Results may differ from a plain program's by a relative error of at most 0.012.
Values may be sent and summed in bfloat16 or wider, within the bound.
A program may use at most 128 MiB of HBM per device.

v0:
```python
import jax
import jax.numpy as jnp
from jax import lax
from jax.sharding import PartitionSpec as P

HEAD_DIM = 128


def carried_in(value, axis, combine, identity):
    peers, place = (lax.axis_size(axis), lax.axis_index(axis))
    everything = lax.all_gather(value.astype(jnp.bfloat16), axis)
    start = jnp.broadcast_to(jnp.asarray(identity, value.dtype), value.shape)

    def step(k, before):
        at = peers - 1 - k
        reached = at > place
        new = combine(before, everything[at].astype(value.dtype))
        return jnp.where(reached, new, before)

    return lax.fori_loop(0, peers, step, start)


def add_states(earlier, later_part):
    return earlier + later_part


def split_heads(matrix, head_dim):
    return matrix.reshape(matrix.shape[0], matrix.shape[1] // head_dim, head_dim)


def on_device(query, key_in, value, gate, gain, grad_out):
    head_dim = HEAD_DIM
    tok_here = query.shape[0]
    queries = split_heads(query, head_dim)
    keys_here = split_heads(key_in, head_dim)
    values_here = split_heads(value, head_dim)
    local_state = jnp.einsum(
        "thd,the->hde", keys_here, values_here, preferred_element_type=jnp.float32
    )
    zero_state = jnp.zeros_like(local_state)
    my_index = lax.axis_index("seq")
    shard_piece = lax.all_gather(
        local_state[None].astype(jnp.bfloat16), "seq", axis=0, tiled=True
    ).astype(jnp.float32)
    position = jnp.arange(shard_piece.shape[0], dtype=jnp.int32)
    keep_rows = (position < my_index).astype(jnp.float32)
    prefix = zero_state + jnp.sum(keep_rows[:, None, None, None] * shard_piece, axis=0)
    causal = jnp.tril(jnp.ones((tok_here, tok_here), dtype=bool))
    scores = jnp.einsum("thd,shd->hts", queries, keys_here, preferred_element_type=jnp.float32)
    masked_scores = jnp.where(causal[None], scores, 0.0).astype(jnp.bfloat16)
    prefix_low = prefix.astype(jnp.bfloat16)
    attn_out = jnp.einsum(
        "hts,she->the", masked_scores, values_here, preferred_element_type=jnp.float32
    )
    attn_out = attn_out + jnp.einsum(
        "thd,hde->the", queries, prefix_low, preferred_element_type=jnp.float32
    )
    attn_out = attn_out.astype(jnp.bfloat16).reshape(tok_here, -1)
    token_rows = lax.all_to_all(attn_out, "head", split_axis=0, concat_axis=1, tiled=True)
    rows_wide = token_rows.astype(jnp.float32)
    inv_rms = lax.rsqrt(jnp.mean(rows_wide * rows_wide, axis=1, keepdims=True) + 1e-06)
    normed = rows_wide * inv_rms
    gate_wide = gate.astype(jnp.float32)
    sigmoid_gate = jax.nn.sigmoid(gate_wide)
    scaled = grad_out.astype(jnp.float32) * gain[None, :]
    grad_gate = (scaled * normed * sigmoid_gate * (1.0 + gate_wide * (1.0 - sigmoid_gate))).astype(
        jnp.bfloat16
    )
    weighted = scaled * gate_wide * sigmoid_gate
    grad_rows = inv_rms * (weighted - normed * jnp.mean(weighted * normed, axis=1, keepdims=True))
    grad_rows = grad_rows.astype(jnp.bfloat16)
    grad_heads = lax.all_to_all(grad_rows, "head", split_axis=1, concat_axis=0, tiled=True)
    grad_attn = split_heads(grad_heads, head_dim)
    local_grad = jnp.einsum("thd,the->hde", queries, grad_attn, preferred_element_type=jnp.float32)
    suffix = carried_in(local_grad, "seq", add_states, zero_state)
    suffix_low = suffix.astype(jnp.bfloat16)
    grad_scores = jnp.einsum(
        "the,she->hts", grad_attn, values_here, preferred_element_type=jnp.float32
    )
    grad_scores = jnp.where(causal[None], grad_scores, 0.0).astype(jnp.bfloat16)
    grad_query = jnp.einsum(
        "hts,shd->thd", grad_scores, keys_here, preferred_element_type=jnp.float32
    )
    grad_query = grad_query + jnp.einsum(
        "the,hde->thd", grad_attn, prefix_low, preferred_element_type=jnp.float32
    )
    grad_key = jnp.einsum("hts,thd->shd", grad_scores, queries, preferred_element_type=jnp.float32)
    grad_key = grad_key + jnp.einsum(
        "she,hde->shd", values_here, suffix_low, preferred_element_type=jnp.float32
    )
    grad_value = jnp.einsum(
        "hts,the->she", masked_scores, grad_attn, preferred_element_type=jnp.float32
    )
    grad_value = grad_value + jnp.einsum(
        "shd,hde->she", keys_here, suffix_low, preferred_element_type=jnp.float32
    )
    return (
        grad_query.astype(jnp.bfloat16).reshape(tok_here, -1),
        grad_key.astype(jnp.bfloat16).reshape(tok_here, -1),
        grad_value.astype(jnp.bfloat16).reshape(tok_here, -1),
        grad_gate,
    )


def solution(mesh):
    in_specs = (
        P("seq", "head"),
        P("seq", "head"),
        P("seq", "head"),
        P(("seq", "head"), None),
        P(),
        P(("seq", "head"), None),
    )
    out_specs = (P("seq", "head"), P("seq", "head"), P("seq", "head"), P(("seq", "head"), None))
    return jax.shard_map(
        on_device, mesh=mesh, in_specs=in_specs, out_specs=out_specs, check_vma=False
    )
```

profile of v0, /device:TPU:0, one launch (start us, length us, event | category | flops | bytes accessed | tf_op | source)
XLA Modules:
  0.0 316.0 jit_solution(6141891403211392233)
XLA Ops:
  7.2 0.0 copy-start
  7.2 0.0 all-gather.5.cloned.1.call-start
  7.2 3.7 %copy.120 = bf16[64,8,16,128]{3,2,1,0:T(8,128)(2,1)} copy(bf16[64,8,16,128]{3,1,2,0:T(8,128)(2,1)} %bitcast.129) | data formatting | bytes 4194304
  10.9 4.3 %copy.88 = bf16[512,16,128]{0,2,1:T(8,128)(2,1)} copy(bf16[512,16,128]{2,1,0:T(8,128)(2,1)} %bitcast.128) | data formatting | bytes 4194304 | tf_op jit(solution)/shard_map/reshape | solution.py:28
  15.2 0.0 copy-done
  15.2 3.1 fusion.39
  18.3 0.0 all-gather.5.cloned.1.call-update
  18.3 0.1 iota_compare_fusion
  18.4 4.6 %select_convert_fusion.1 = bf16[16,512,512]{2,1,0:T(8,128)(2,1)S(1)} fusion(pred[512,512]{1,0:T(8,128)(4,1)S(1)} %iota_compare_fusion, bf16[512,2048]{1,0:T(8,128)(2,1)} %param.9, bf16[512,2048]{1,0:T(8,128)(2,1)} %param.8), kind=kOutput, calls=%fused_computation.2 | convolution fusion | flops 1082130432 | bytes 12845056 | tf_op jit(solution)/shard_map/thd,shd->hts/dot_general | solution.py:49
  23.0 0.0 copy-start.1
  23.1 3.2 %copy-done.1 = bf16[16,512,512]{2,1,0:T(8,128)(2,1)} copy-done((bf16[16,512,512]{2,1,0:T(8,128)(2,1)}, bf16[16,512,512]{2,1,0:T(8,128)(2,1)S(1)}, u32[]{:S(2)}) %copy-start.1) | copy-done | bytes 8388632
  26.3 4.3 %fusion.17 = f32[16,512,128]{2,1,0:T(8,128)} fusion(bf16[16,512,512]{2,1,0:T(8,128)(2,1)S(1)} %select_convert_fusion.1, bf16[512,2048]{1,0:T(8,128)(2,1)S(1)} %copy-done), kind=kOutput, calls=%fused_computation.34 | convolution fusion | flops 1073741824 | bytes 14680064 | tf_op jit(solution)/shard_map/hts,she->the/dot_general | solution.py:52
  30.6 63.4 %all-gather.5.cloned.1.call-done = bf16[128,128,128]{2,1,0:T(8,128)(2,1)} async-done(((bf16[16,128,128]{2,1,0:T(8,128)(2,1)}), bf16[128,128,128]{2,1,0:T(8,128)(2,1)}) %all-gather.5.cloned.1.call-update) | async-done | bytes 4194320 | tf_op jit(solution)/shard_map/all_gather | solution.py:42
  94.0 3.3 %fusion = bf16[16,128,128]{2,1,0:T(8,128)(2,1)S(1)} fusion(bf16[8,16,128,128]{3,2,1,0:T(8,128)(2,1)} %bitcast.132, f32[8]{0:T(128)S(1)} %compare_convert_fusion), kind=kLoop, calls=%fused_computation.4 | loop fusion | flops 6029312 | bytes 4718624 | tf_op jit(solution)/shard_map/reduce_sum | solution.py:47
  97.3 0.2 copy-done.8
  97.4 2.5 fusion.11
  99.9 0.0 copy-done.11
  99.9 2.7 copy.93
  102.6 4.2 %all_to_all.22 = bf16[4,128,2048]{2,1,0:T(8,128)(2,1)} reshape(bf16[512,16,128]{2,1,0:T(8,128)(2,1)} %copy.93) | data formatting | bytes 4194304 | tf_op jit(solution)/shard_map/all_to_all | solution.py:59
  106.8 4.5 %all-to-all-start = ((bf16[4,128,2048]{2,1,0:T(8,128)(2,1)}), bf16[4,128,2048]{2,1,0:T(8,128)(2,1)}, u32[]{:S(2)}, u32[]{:S(2)}) async-start(bf16[4,128,2048]{2,1,0:T(8,128)(2,1)} %all_to_all.22), calls=%async_computation | async-start | bytes 4194304 | tf_op jit(solution)/shard_map/all_to_all | solution.py:59
  111.2 0.2 all-gather.7.cloned.1.call-start
  111.5 4.1 %copy.95 = bf16[128,8192]{0,1:T(8,128)(2,1)} copy(bf16[128,8192]{1,0:T(8,128)(2,1)} %param.11) | data formatting | bytes 4194304 | tf_op args[3]
  115.5 4.1 %copy.94 = bf16[128,8192]{0,1:T(8,128)(2,1)} copy(bf16[128,8192]{1,0:T(8,128)(2,1)} %param.13) | data formatting | bytes 4194304 | tf_op args[5]
  119.6 17.4 %all-to-all-done = bf16[4,128,2048]{2,1,0:T(8,128)(2,1)} async-done(((bf16[4,128,2048]{2,1,0:T(8,128)(2,1)}), bf16[4,128,2048]{2,1,0:T(8,128)(2,1)}, u32[]{:S(2)}, u32[]{:S(2)}) %all-to-all-start) | async-done | bytes 2097184 | tf_op jit(solution)/shard_map/all_to_all | solution.py:59
  137.0 2.1 fusion.1
  139.0 4.1 %convert_bitcast_fusion = f32[128,4,2048]{2,0,1:T(8,128)} fusion(bf16[4,128,2048]{2,1,0:T(8,128)(2,1)} %all-to-all-done), kind=kLoop, calls=%fused_computation.8 | loop fusion | flops 1048576 | bytes 6291456 | tf_op jit(solution)/shard_map/convert_element_type | solution.py:60
  143.1 5.4 %copy.96 = f32[128,4,2048]{0,2,1:T(8,128)} copy(f32[128,4,2048]{2,0,1:T(8,128)} %convert_bitcast_fusion) | data formatting | bytes 8388608 | tf_op jit(solution)/shard_map/convert_element_type | solution.py:60
  148.5 0.0 copy-done.12
  148.5 0.0 copy-start.7
  148.5 6.7 %multiply_reduce_fusion = f32[128]{0:T(128)S(1)} fusion(f32[128,4,2048]{0,2,1:T(8,128)} %copy.96, f32[128]{0:T(128)S(1)} %add_rsqrt_fusion, bf16[128,8192]{0,1:T(8,128)(2,1)} %copy.95, f32[8192]{0:T(1024)S(1)} %copy-done.12, bf16[128,8192]{0,1:T(8,128)(2,1)} %copy.94), kind=kLoop, calls=%fused_computation.27 | loop fusion | flops 11534208 | bytes 8422400 | tf_op jit(solution)/shard_map/reduce_sum | solution.py:70
  155.3 4.4 %fusion.8 = (bf16[128,8192]{0,1:T(8,128)(2,1)}, bf16[128,8192]{0,1:T(8,128)(2,1)}) fusion(bf16[128,8192]{0,1:T(8,128)(2,1)S(1)} %copy-done.6, bf16[128,8192]{0,1:T(8,128)(2,1)S(1)} %copy-done.7, f32[128,4,2048]{0,2,1:T(8,128)S(1)} %copy-done.2, f32[8192]{0:T(1024)S(1)} %copy-done.12, f32[128]{0:T(128)S(1)} %add_rsqrt_fusion, f32[128]{0:T(128)S(1)} %broadcast_multiply_fusion), kind=kLoop, calls=%fused_computation.17 | loop fusion | flops 20971520 | bytes 12616704 | tf_op jit(solution)/shard_map/convert_element_type | solution.py:66
  159.7 3.9 %copy.97 = bf16[128,4,2048]{2,0,1:T(8,128)(2,1)} copy(bf16[128,4,2048]{0,2,1:T(8,128)(2,1)} %bitcast.124) | data formatting | bytes 4194304 | tf_op jit(solution)/shard_map/all_to_all | solution.py:72
  163.7 29.2 %all_to_all.29 = bf16[128,4,2048]{2,0,1:T(8,128)(2,1)S(1)} all-to-all(bf16[128,4,2048]{2,0,1:T(8,128)(2,1)} %copy.97), channel_id=1, replica_groups=mesh['seq'=8,'head'=4] {'head'}, dimensions={1} | all-to-all | bytes 4194304 | tf_op jit(solution)/shard_map/all_to_all | solution.py:72
  192.9 2.0 copy.121
  194.9 4.3 %copy.103 = bf16[512,16,128]{0,2,1:T(8,128)(2,1)} copy(bf16[512,16,128]{2,1,0:T(8,128)(2,1)} %bitcast.127) | data formatting | bytes 4194304 | tf_op jit(solution)/shard_map/reshape | solution.py:28
  199.2 2.9 fusion.42
  202.1 1.0 copy.105
  203.2 0.0 all-gather.7.cloned.1.call-update
  203.2 4.1 %copy.113 = bf16[128,8192]{1,0:T(8,128)(2,1)} copy(bf16[128,8192]{0,1:T(8,128)(2,1)} %get-tuple-element.166) | data formatting | bytes 4194304
  207.3 4.4 %select_convert_fusion = bf16[16,512,512]{2,1,0:T(8,128)(2,1)S(1)} fusion(bf16[512,16,128]{0,2,1:T(8,128)(2,1)} %copy.103, pred[512,512]{1,0:T(8,128)(4,1)S(1)} %iota_compare_fusion, bf16[512,2048]{1,0:T(8,128)(2,1)S(1)} %copy-done), kind=kOutput, calls=%fused_computation.1 | convolution fusion | flops 1082130432 | bytes 12845056 | tf_op jit(solution)/shard_map/the,she->hts/dot_general | solution.py:77
  211.7 4.8 %fusion.49 = f32[16,512,128]{1,2,0:T(8,128)} fusion(bf16[16,512,512]{2,1,0:T(8,128)(2,1)S(1)} %select_convert_fusion, bf16[512,16,128]{0,2,1:T(8,128)(2,1)S(1)} %copy-done.9), kind=kOutput, calls=%fused_computation.64 | convolution fusion | flops 1073741824 | bytes 14680064 | tf_op jit(solution)/shard_map/hts,shd->thd/dot_general | solution.py:81
  216.5 0.0 copy-done.3
  216.5 0.0 copy-done.5
  216.5 4.5 %fusion.10 = bf16[512,16,128]{0,2,1:T(8,128)(2,1)} fusion(f32[16,512,128]{1,2,0:T(8,128)} %fusion.49, bf16[512,16,128]{0,2,1:T(8,128)(2,1)S(1)} %copy-done.5, bf16[16,128,128]{2,1,0:T(8,128)(2,1)} %copy-done.11), kind=kOutput, calls=%fused_computation.21 | convolution fusion | flops 270532608 | bytes 8912896 | tf_op jit(solution)/shard_map/the,hde->thd/dot_general | solution.py:84
  221.0 3.9 %copy.110 = bf16[512,2048]{1,0:T(8,128)(2,1)} copy(bf16[512,2048]{0,1:T(8,128)(2,1)} %bitcast.125) | data formatting | bytes 4194304
  224.9 7.3 %fusion.50 = f32[16,128,512]{2,1,0:T(8,128)} fusion(bf16[512,16,128]{0,2,1:T(8,128)(2,1)} %copy.103, bf16[16,512,512]{2,1,0:T(8,128)(2,1)} %copy-done.1), kind=kOutput, calls=%fused_computation.65 | convolution fusion | flops 1073741824 | bytes 14680064 | tf_op jit(solution)/shard_map/hts,the->she/dot_general | solution.py:91
  232.2 41.6 %all-gather.7.cloned.1.call-done = bf16[128,128,128]{2,1,0:T(8,128)(2,1)} async-done(((bf16[16,128,128]{2,1,0:T(8,128)(2,1)}), bf16[128,128,128]{2,1,0:T(8,128)(2,1)}) %all-gather.7.cloned.1.call-update) | async-done | bytes 4194320 | tf_op jit(solution)/shard_map/all_gather | solution.py:11
  273.8 13.1 %while.16 = (s32[]{:T(128)}, f32[16,128,128]{2,1,0:T(8,128)S(1)}, s32[]{:T(128)}, bf16[8,16,128,128]{3,2,1,0:T(8,128)(2,1)}, s32[]{:T(128)}, /*index=5*/s32[]{:T(128)}, s32[]{:T(128)}, s32[]{:T(128)}) while((s32[]{:T(128)}, f32[16,128,128]{2,1,0:T(8,128)S(1)}, s32[]{:T(128)}, bf16[8,16,128,128]{3,2,1,0:T(8,128)(2,1)}, s32[]{:T(128)}, ...), condition=%wide.region_4.5_spmd.clone, body=%wide.region_3.4_spmd.clone.sunk | while | flops 1048584 | bytes 2621603 | solution.py:20
  273.8 1.6 add_select_fusion.2
  275.4 1.6 add_select_fusion.2
  277.0 1.6 add_select_fusion.2
  278.7 1.6 add_select_fusion.2
  280.3 1.6 add_select_fusion.2
  282.0 1.6 add_select_fusion.2
  283.6 1.6 add_select_fusion.2
  285.3 1.6 add_select_fusion.2
  286.9 0.0 copy-start.10
  286.9 2.9 fusion.12
  289.8 0.6 copy-done.4
  290.3 0.9 copy-done.10
  291.3 2.2 add_convert_fusion
  293.4 3.9 %copy.112 = bf16[512,2048]{1,0:T(8,128)(2,1)} copy(bf16[512,2048]{0,1:T(8,128)(2,1)} %bitcast.130) | data formatting | bytes 4194304
  297.3 7.9 %fusion.9 = bf16[512,16,128]{0,2,1:T(8,128)(2,1)} fusion(f32[16,128,512]{2,1,0:T(8,128)} %fusion.12, bf16[16,512,512]{2,1,0:T(8,128)(2,1)} %copy-done.3, bf16[512,2048]{1,0:T(8,128)(2,1)} %param.8), kind=kOutput, calls=%fused_computation.19 | convolution fusion | flops 1075838976 | bytes 16777216 | tf_op jit(solution)/shard_map/hts,thd->shd/dot_general | solution.py:87
  305.3 3.9 %copy.111 = bf16[512,2048]{1,0:T(8,128)(2,1)} copy(bf16[512,2048]{0,1:T(8,128)(2,1)} %bitcast.131) | data formatting | bytes 4194304
  (17 shorter events, 0.0 us)
Async XLA Ops:
  7.2 8.0 %copy-start = (bf16[512,2048]{1,0:T(8,128)(2,1)S(1)}, bf16[512,2048]{1,0:T(8,128)(2,1)}, u32[]{:S(2)}) copy-start(bf16[512,2048]{1,0:T(8,128)(2,1)} %param.10) | copy-start | bytes 6291460
  7.2 86.8 %all-gather.5.cloned.1.call-start = ((), (), s32[]{:S(2)}) async-start(), calls=%async_computation.2 | async-start | bytes 4718592 | tf_op jit(solution)/shard_map/all_gather | solution.py:42
  23.0 3.2 %copy-start.1 = (bf16[16,512,512]{2,1,0:T(8,128)(2,1)}, bf16[16,512,512]{2,1,0:T(8,128)(2,1)S(1)}, u32[]{:S(2)}) copy-start(bf16[16,512,512]{2,1,0:T(8,128)(2,1)S(1)} %select_convert_fusion.1) | copy-start | bytes 25165828
  94.0 3.4 %copy-start.8 = (f32[16,512,128]{2,1,0:T(8,128)S(1)}, f32[16,512,128]{2,1,0:T(8,128)}, u32[]{:S(2)}) copy-start(f32[16,512,128]{2,1,0:T(8,128)} %fusion.17) | copy-start | bytes 12582916
  97.4 2.5 copy-start.11
  106.8 30.2 %all-to-all-start = ((bf16[4,128,2048]{2,1,0:T(8,128)(2,1)}), bf16[4,128,2048]{2,1,0:T(8,128)(2,1)}, u32[]{:S(2)}, u32[]{:S(2)}) async-start(bf16[4,128,2048]{2,1,0:T(8,128)(2,1)} %all_to_all.22), calls=%async_computation | async-start | bytes 4194304 | tf_op jit(solution)/shard_map/all_to_all | solution.py:59
  111.2 162.5 %all-gather.7.cloned.1.call-start = ((), (), s32[]{:S(2)}) async-start(), calls=%async_computation.3 | async-start | bytes 4718592 | tf_op jit(solution)/shard_map/all_gather | solution.py:11
  143.1 5.4 %copy-start.12 = (f32[8192]{0:T(1024)S(1)}, f32[8192]{0:T(1024)}, u32[]{:S(2)}) copy-start(f32[8192]{0:T(1024)} %param.12) | copy-start | bytes 98308
  148.5 6.8 %copy-start.2 = (f32[128,4,2048]{0,2,1:T(8,128)S(1)}, f32[128,4,2048]{0,2,1:T(8,128)}, u32[]{:S(2)}) copy-start(f32[128,4,2048]{0,2,1:T(8,128)} %copy.96) | copy-start | bytes 12582916
  148.5 6.8 %copy-start.6 = (bf16[128,8192]{0,1:T(8,128)(2,1)S(1)}, bf16[128,8192]{0,1:T(8,128)(2,1)}, u32[]{:S(2)}) copy-start(bf16[128,8192]{0,1:T(8,128)(2,1)} %copy.95) | copy-start | bytes 6291460
  148.5 6.8 %copy-start.7 = (bf16[128,8192]{0,1:T(8,128)(2,1)S(1)}, bf16[128,8192]{0,1:T(8,128)(2,1)}, u32[]{:S(2)}) copy-start(bf16[128,8192]{0,1:T(8,128)(2,1)} %copy.94) | copy-start | bytes 6291460
  207.3 4.4 %copy-start.9 = (bf16[512,16,128]{0,2,1:T(8,128)(2,1)S(1)}, bf16[512,16,128]{0,2,1:T(8,128)(2,1)}, u32[]{:S(2)}) copy-start(bf16[512,16,128]{0,2,1:T(8,128)(2,1)} %copy.88) | copy-start | bytes 6291460
  211.7 4.8 %copy-start.3 = (bf16[16,512,512]{2,1,0:T(8,128)(2,1)}, bf16[16,512,512]{2,1,0:T(8,128)(2,1)S(1)}, u32[]{:S(2)}) copy-start(bf16[16,512,512]{2,1,0:T(8,128)(2,1)S(1)} %select_convert_fusion) | copy-start | bytes 25165828
  211.7 4.8 %copy-start.5 = (bf16[512,16,128]{0,2,1:T(8,128)(2,1)S(1)}, bf16[512,16,128]{0,2,1:T(8,128)(2,1)}, u32[]{:S(2)}) copy-start(bf16[512,16,128]{0,2,1:T(8,128)(2,1)} %copy.103) | copy-start | bytes 6291460
  286.9 3.4 %copy-start.4 = (f32[16,128,512]{2,1,0:T(8,128)S(1)}, f32[16,128,512]{2,1,0:T(8,128)}, u32[]{:S(2)}) copy-start(f32[16,128,512]{2,1,0:T(8,128)} %fusion.50) | copy-start | bytes 12582916
  286.9 4.4 %copy-start.10 = (bf16[512,2048]{1,0:T(8,128)(2,1)S(1)}, bf16[512,2048]{1,0:T(8,128)(2,1)}, u32[]{:S(2)}) copy-start(bf16[512,2048]{1,0:T(8,128)(2,1)} %param.9) | copy-start | bytes 6291460
Sparse Core Ops, SparseCore 0:
  18.4 75.5 all-gather.4
  203.3 70.4 all-gather.6
where the time goes:
time: 318 us; the launch traced here: 316 us
  waiting for transfers between devices  122 us (38%)
  local copies, waits for them, and re-layouts  60.3 us (19%)
  matrix products  51.3 us (16%)
  other arithmetic  33.6 us (11%)
  blocking collectives  29.2 us (9%)
  between operations  14.2 us (4%)
  starting transfers between devices  4.72 us (1%)
    all_gather x1, waiting for transfers between devices, on_device(): lax.all_gather(local_state[None].astype(jnp.bfloat16), 'seq', axis=0, til...  63.4 us
    all_gather x1, waiting for transfers between devices, carried_in(): everything = lax.all_gather(value.astype(jnp.bfloat16), axis)  41.6 us
    unnamed x34, local copies, waits for them, and re-layouts  34.6 us
    all_to_all x1, blocking collectives, on_device(): lax.all_to_all(grad_rows, 'head', split_axis=1, concat_axis=0, tiled=True)  29.2 us
    all_to_all x1, waiting for transfers between devices, on_device(): lax.all_to_all(attn_out, 'head', split_axis=0, concat_axis=1, tiled=True)  17.4 us
    select_n x8, other arithmetic, step(): return jnp.where(reached, new, before)  12.9 us
    reshape x2, local copies, waits for them, and re-layouts, split_heads(): matrix.reshape(matrix.shape[0], matrix.shape[1] // head_dim, head_dim)  8.6 us
    dot_general x1, matrix products, on_device(): jnp.einsum('hts,thd->shd', grad_scores, queries, preferred_element_type=j...  7.93 us
  transfers between devices with their start and end apart: 3, of which 3 were waited for; matrix products, arithmetic and copies ran while one was open for 15% of the time, Pallas kernels for 0%

commit v1 on v0

--- a/solution.py
+++ b/solution.py
@@ -56,7 +56,10 @@
         "thd,hde->the", queries, prefix_low, preferred_element_type=jnp.float32
     )
     attn_out = attn_out.astype(jnp.bfloat16).reshape(tok_here, -1)
-    token_rows = lax.all_to_all(attn_out, "head", split_axis=0, concat_axis=1, tiled=True)
+    token_rows = jnp.concatenate(
+        lax.all_to_all(jnp.stack(jnp.split(attn_out, lax.axis_size("head"), axis=0)), "head", 0, 0),
+        axis=1,
+    )
     rows_wide = token_rows.astype(jnp.float32)
     inv_rms = lax.rsqrt(jnp.mean(rows_wide * rows_wide, axis=1, keepdims=True) + 1e-06)
     normed = rows_wide * inv_rms

time: 318 us -> 300 us (0.943)
  blocking collectives: 29.2 us -> 56.3 us
  local copies, waits for them, and re-layouts: 60.3 us -> 39.1 us
  waiting for transfers between devices: 122 us -> 109 us
  starting transfers between devices: 4.72 us -> 0.08 us
  other arithmetic: 33.6 us -> 29 us
    all_to_all x0 -> x1, blocking collectives: none -> 28.2 us  [on_device(): lax.all_to_all(jnp.stack(jnp.split(attn_out, lax.axis_size('head'), axis=...]
    all_to_all x1 -> x0, waiting for transfers between devices: 17.4 us -> none  [on_device(): lax.all_to_all(attn_out, 'head', split_axis=0, concat_axis=1, tiled=True)]
    unnamed x34 -> x31, local copies, waits for them, and re-layouts: 34.6 us -> 23 us
    all_to_all x1 -> x0, starting transfers between devices: 4.46 us -> none  [on_device(): lax.all_to_all(attn_out, 'head', split_axis=0, concat_axis=1, tiled=True)]
    all_to_all x1 -> x0, local copies, waits for them, and re-layouts: 4.15 us -> none  [on_device(): lax.all_to_all(attn_out, 'head', split_axis=0, concat_axis=1, tiled=True)]
    all_gather x1, waiting for transfers between devices: 41.6 us -> 45.7 us  [carried_in(): everything = lax.all_gather(value.astype(jnp.bfloat16), axis)]
    all_to_all x1, local copies, waits for them, and re-layouts: 3.94 us -> 0.24 us  [on_device(): lax.all_to_all(grad_rows, 'head', split_axis=1, concat_axis=0, tiled=True)]
  transfers between devices with their start and end apart: 3 -> 2, of which waited for: 3 -> 2; matrix products, arithmetic and copies ran while one was open for 15% -> 11% of each run, Pallas kernels for 0% -> 0%
where the time goes in v1:
time: 300 us; the launch traced here: 299 us
  waiting for transfers between devices  109 us (36%)
  blocking collectives  56.3 us (19%)
  matrix products  51.8 us (17%)
  local copies, waits for them, and re-layouts  39.1 us (13%)
  other arithmetic  29 us (10%)
  between operations  14.2 us (5%)
    all_gather x1, waiting for transfers between devices, on_device(): lax.all_gather(local_state[None].astype(jnp.bfloat16), 'seq', axis=0, til...  62.8 us
    all_gather x1, waiting for transfers between devices, carried_in(): everything = lax.all_gather(value.astype(jnp.bfloat16), axis)  45.7 us
    all_to_all x1, blocking collectives, on_device(): lax.all_to_all(jnp.stack(jnp.split(attn_out, lax.axis_size('head'), axis=...  28.2 us
    all_to_all x1, blocking collectives, on_device(): lax.all_to_all(grad_rows, 'head', split_axis=1, concat_axis=0, tiled=True)  28.1 us
    unnamed x31, local copies, waits for them, and re-layouts  23 us
    select_n x8, other arithmetic, step(): return jnp.where(reached, new, before)  12.9 us
    reshape x2, local copies, waits for them, and re-layouts, split_heads(): matrix.reshape(matrix.shape[0], matrix.shape[1] // head_dim, head_dim)  8.61 us
    dot_general x1, matrix products, on_device(): jnp.einsum('hts,thd->shd', grad_scores, queries, preferred_element_type=j...  7.93 us
  transfers between devices with their start and end apart: 2, of which 2 were waited for; matrix products, arithmetic and copies ran while one was open for 11% of the time, Pallas kernels for 0%

profile of v1, /device:TPU:0, one launch (start us, length us, event | category | flops | bytes accessed | tf_op | source)
XLA Modules:
  0.0 299.3 jit_solution(2461580072358476877)
XLA Ops:
  7.2 0.0 copy-start
  7.2 0.0 all-gather.5.cloned.1.call-start
  7.2 3.7 %copy.86 = bf16[64,8,16,128]{3,2,1,0:T(8,128)(2,1)} copy(bf16[64,8,16,128]{3,1,2,0:T(8,128)(2,1)} %bitcast.131) | data formatting | bytes 4194304
  10.9 4.3 %copy.58 = bf16[512,16,128]{0,2,1:T(8,128)(2,1)} copy(bf16[512,16,128]{2,1,0:T(8,128)(2,1)} %bitcast.130) | data formatting | bytes 4194304 | tf_op jit(solution)/shard_map/reshape | solution.py:28
  15.2 0.0 copy-done
  15.2 3.1 %fusion.38 = bf16[16,128,128]{2,1,0:T(8,128)(2,1)} fusion(bf16[512,16,128]{0,2,1:T(8,128)(2,1)} %copy.58, bf16[512,2048]{1,0:T(8,128)(2,1)S(1)} %copy-done), kind=kOutput, calls=%fused_computation.53 | convolution fusion | flops 268697600 | bytes 4718592 | tf_op jit(solution)/shard_map/thd,the->hde/dot_general | solution.py:37
  18.3 0.0 all-gather.5.cloned.1.call-update
  18.3 0.0 all-gather.7.cloned.1.call-start
  18.4 0.1 iota_compare_fusion
  18.5 4.6 %select_convert_fusion.1 = bf16[16,512,512]{2,1,0:T(8,128)(2,1)S(1)} fusion(pred[512,512]{1,0:T(8,128)(4,1)S(1)} %iota_compare_fusion, bf16[512,2048]{1,0:T(8,128)(2,1)} %param.9, bf16[512,2048]{1,0:T(8,128)(2,1)} %param.8), kind=kOutput, calls=%fused_computation.2 | convolution fusion | flops 1082130432 | bytes 12845056 | tf_op jit(solution)/shard_map/thd,shd->hts/dot_general | solution.py:49
  23.1 0.0 copy-start.1
  23.1 3.2 %copy-done.1 = bf16[16,512,512]{2,1,0:T(8,128)(2,1)} copy-done((bf16[16,512,512]{2,1,0:T(8,128)(2,1)}, bf16[16,512,512]{2,1,0:T(8,128)(2,1)S(1)}, u32[]{:S(2)}) %copy-start.1) | copy-done | bytes 8388632
  26.3 4.8 %fusion.11 = f32[16,512,128]{1,2,0:T(8,128)} fusion(bf16[16,512,512]{2,1,0:T(8,128)(2,1)S(1)} %select_convert_fusion.1, bf16[512,2048]{1,0:T(8,128)(2,1)S(1)} %copy-done), kind=kOutput, calls=%fused_computation.27 | convolution fusion | flops 1073741824 | bytes 14680064 | tf_op jit(solution)/shard_map/hts,she->the/dot_general | solution.py:52
  31.2 62.8 %all-gather.5.cloned.1.call-done = bf16[128,128,128]{2,1,0:T(8,128)(2,1)} async-done(((bf16[16,128,128]{2,1,0:T(8,128)(2,1)}), bf16[128,128,128]{2,1,0:T(8,128)(2,1)}) %all-gather.5.cloned.1.call-update) | async-done | bytes 4194320 | tf_op jit(solution)/shard_map/all_gather | solution.py:42
  94.0 3.3 %fusion = bf16[16,128,128]{2,1,0:T(8,128)(2,1)S(1)} fusion(bf16[8,16,128,128]{3,2,1,0:T(8,128)(2,1)} %bitcast.134, f32[8]{0:T(128)S(1)} %compare_convert_fusion), kind=kLoop, calls=%fused_computation.4 | loop fusion | flops 6029312 | bytes 4718624 | tf_op jit(solution)/shard_map/reduce_sum | solution.py:47
  97.3 0.2 copy-done.6
  97.4 2.6 fusion.10
  100.0 0.0 copy-done.11
  100.0 0.6 fusion.48
  100.6 0.3 pad_maximum_fusion
  100.9 28.2 %all_to_all.21 = bf16[4,128,2048]{1,2,0:T(8,128)(2,1)S(1)} all-to-all(bf16[4,128,2048]{1,2,0:T(8,128)(2,1)S(1)} %pad_maximum_fusion), channel_id=1, replica_groups=mesh['seq'=8,'head'=4] {'head'}, dimensions={0} | all-to-all | bytes 4194304 | tf_op jit(solution)/shard_map/all_to_all | solution.py:60
  129.1 1.1 multiply_reduce_fusion.1
  130.2 2.2 convert_element_type.94
  132.4 5.6 %copy.81 = f32[128,8192]{1,0:T(8,128)} copy(f32[128,8192]{0,1:T(8,128)} %bitcast.124) | data formatting | bytes 8388608 | tf_op jit(solution)/shard_map/convert_element_type | solution.py:63
  138.1 0.0 copy-done.12
  138.1 0.0 copy-start.8
  138.1 5.3 %multiply_reduce_fusion = f32[128]{0:T(128)S(1)} fusion(f32[128,8192]{1,0:T(8,128)} %copy.81, f32[128]{0:T(128)S(1)} %add_rsqrt_fusion, bf16[128,8192]{1,0:T(8,128)(2,1)} %param.11, f32[8192]{0:T(1024)S(1)} %copy-done.12, bf16[128,8192]{1,0:T(8,128)(2,1)} %param.13), kind=kLoop, calls=%fused_computation.23 | loop fusion | flops 11534208 | bytes 8422400 | tf_op jit(solution)/shard_map/reduce_sum | solution.py:73
  143.4 0.0 copy-done.2
  143.4 0.0 copy-done.7
  143.4 0.6 copy-done.8
  144.0 3.8 %fusion.7 = (bf16[128,8192]{1,0:T(8,128)(2,1)}, bf16[128,8192]{1,0:T(8,128)(2,1)S(1)}) fusion(bf16[128,8192]{1,0:T(8,128)(2,1)S(1)} %copy-done.7, bf16[128,8192]{1,0:T(8,128)(2,1)S(1)} %copy-done.8, f32[128,8192]{1,0:T(8,128)S(1)} %copy-done.2, f32[8192]{0:T(1024)S(1)} %copy-done.12, f32[128]{0:T(128)S(1)} %add_rsqrt_fusion, f32[128]{0:T(128)S(1)} %broadcast_multiply_fusion), kind=kLoop, calls=%fused_computation.14 | loop fusion | flops 20971520 | bytes 12616704 | tf_op jit(solution)/shard_map/convert_element_type | solution.py:69
  147.8 0.2 copy.135
  148.0 28.1 %all_to_all.22 = bf16[128,4,2048]{2,0,1:T(8,128)(2,1)S(1)} all-to-all(bf16[128,4,2048]{2,0,1:T(8,128)(2,1)S(1)} %bitcast.127), channel_id=1, replica_groups=mesh['seq'=8,'head'=4] {'head'}, dimensions={1} | all-to-all | bytes 4194304 | tf_op jit(solution)/shard_map/all_to_all | solution.py:75
  176.2 2.0 copy.87
  178.1 4.3 %copy.69 = bf16[512,16,128]{0,2,1:T(8,128)(2,1)} copy(bf16[512,16,128]{2,1,0:T(8,128)(2,1)} %bitcast.129) | data formatting | bytes 4194304 | tf_op jit(solution)/shard_map/reshape | solution.py:28
  182.5 2.9 fusion.41
  185.4 1.0 copy.71
  186.4 0.0 all-gather.7.cloned.1.call-update
  186.5 0.0 copy-start.9
  186.5 4.2 %select_convert_fusion = bf16[16,512,512]{2,1,0:T(8,128)(2,1)S(1)} fusion(bf16[512,16,128]{0,2,1:T(8,128)(2,1)} %copy.69, pred[512,512]{1,0:T(8,128)(4,1)S(1)} %iota_compare_fusion, bf16[512,2048]{1,0:T(8,128)(2,1)S(1)} %copy-done), kind=kOutput, calls=%fused_computation.1 | convolution fusion | flops 1082130432 | bytes 12845056 | tf_op jit(solution)/shard_map/the,she->hts/dot_general | solution.py:80
  190.8 4.8 %fusion.49 = f32[16,512,128]{1,2,0:T(8,128)} fusion(bf16[16,512,512]{2,1,0:T(8,128)(2,1)S(1)} %select_convert_fusion, bf16[512,16,128]{0,2,1:T(8,128)(2,1)S(1)} %copy-done.9), kind=kOutput, calls=%fused_computation.64 | convolution fusion | flops 1073741824 | bytes 14680064 | tf_op jit(solution)/shard_map/hts,shd->thd/dot_general | solution.py:84
  195.5 0.1 copy-done.3
  195.6 0.0 copy-done.5
  195.6 4.4 %fusion.9 = bf16[512,16,128]{0,2,1:T(8,128)(2,1)} fusion(f32[16,512,128]{1,2,0:T(8,128)} %fusion.49, bf16[512,16,128]{0,2,1:T(8,128)(2,1)S(1)} %copy-done.5, bf16[16,128,128]{2,1,0:T(8,128)(2,1)} %copy-done.11), kind=kOutput, calls=%fused_computation.18 | convolution fusion | flops 270532608 | bytes 8912896 | tf_op jit(solution)/shard_map/the,hde->thd/dot_general | solution.py:87
  200.1 3.9 %copy.76 = bf16[512,2048]{1,0:T(8,128)(2,1)} copy(bf16[512,2048]{0,1:T(8,128)(2,1)} %bitcast.126) | data formatting | bytes 4194304
  204.0 7.3 %fusion.50 = f32[16,128,512]{2,1,0:T(8,128)} fusion(bf16[512,16,128]{0,2,1:T(8,128)(2,1)} %copy.69, bf16[16,512,512]{2,1,0:T(8,128)(2,1)} %copy-done.1), kind=kOutput, calls=%fused_computation.65 | convolution fusion | flops 1073741824 | bytes 14680064 | tf_op jit(solution)/shard_map/hts,the->she/dot_general | solution.py:94
  211.3 45.7 %all-gather.7.cloned.1.call-done = bf16[128,128,128]{2,1,0:T(8,128)(2,1)} async-done(((bf16[16,128,128]{2,1,0:T(8,128)(2,1)}), bf16[128,128,128]{2,1,0:T(8,128)(2,1)}) %all-gather.7.cloned.1.call-update) | async-done | bytes 4194320 | tf_op jit(solution)/shard_map/all_gather | solution.py:11
  257.0 13.1 %while.16 = (s32[]{:T(128)}, f32[16,128,128]{2,1,0:T(8,128)S(1)}, s32[]{:T(128)}, bf16[8,16,128,128]{3,2,1,0:T(8,128)(2,1)}, s32[]{:T(128)}, /*index=5*/s32[]{:T(128)}, s32[]{:T(128)}, s32[]{:T(128)}) while((s32[]{:T(128)}, f32[16,128,128]{2,1,0:T(8,128)S(1)}, s32[]{:T(128)}, bf16[8,16,128,128]{3,2,1,0:T(8,128)(2,1)}, s32[]{:T(128)}, ...), condition=%wide.region_4.5_spmd.clone, body=%wide.region_3.4_spmd.clone.sunk | while | flops 1048584 | bytes 2621603 | solution.py:20
  257.0 1.6 add_select_fusion.2
  258.7 1.6 add_select_fusion.2
  260.3 1.6 add_select_fusion.2
  262.0 1.6 add_select_fusion.2
  263.6 1.6 add_select_fusion.2
  265.3 1.6 add_select_fusion.2
  266.9 1.6 add_select_fusion.2
  268.5 1.6 add_select_fusion.2
  270.2 0.0 copy-start.10
  270.2 2.9 fusion.13
  273.1 0.5 copy-done.4
  273.6 1.0 copy-done.10
  274.6 2.2 add_convert_fusion
  276.7 3.9 %copy.78 = bf16[512,2048]{1,0:T(8,128)(2,1)} copy(bf16[512,2048]{0,1:T(8,128)(2,1)} %bitcast.132) | data formatting | bytes 4194304
  280.6 7.9 %fusion.8 = bf16[512,16,128]{0,2,1:T(8,128)(2,1)} fusion(f32[16,128,512]{2,1,0:T(8,128)} %fusion.13, bf16[16,512,512]{2,1,0:T(8,128)(2,1)} %copy-done.3, bf16[512,2048]{1,0:T(8,128)(2,1)} %param.8), kind=kOutput, calls=%fused_computation.16 | convolution fusion | flops 1075838976 | bytes 16777216 | tf_op jit(solution)/shard_map/hts,thd->shd/dot_general | solution.py:90
  288.6 3.9 %copy.77 = bf16[512,2048]{1,0:T(8,128)(2,1)} copy(bf16[512,2048]{0,1:T(8,128)(2,1)} %bitcast.133) | data formatting | bytes 4194304
  (13 shorter events, 0.0 us)
Async XLA Ops:
  7.2 8.0 %copy-start = (bf16[512,2048]{1,0:T(8,128)(2,1)S(1)}, bf16[512,2048]{1,0:T(8,128)(2,1)}, u32[]{:S(2)}) copy-start(bf16[512,2048]{1,0:T(8,128)(2,1)} %param.10) | copy-start | bytes 6291460
  7.2 86.8 %all-gather.5.cloned.1.call-start = ((), (), s32[]{:S(2)}) async-start(), calls=%async_computation.2 | async-start | bytes 4718592 | tf_op jit(solution)/shard_map/all_gather | solution.py:42
  18.3 238.7 %all-gather.7.cloned.1.call-start = ((), (), s32[]{:S(2)}) async-start(), calls=%async_computation.3 | async-start | bytes 4718592 | tf_op jit(solution)/shard_map/all_gather | solution.py:11
  23.1 3.2 %copy-start.1 = (bf16[16,512,512]{2,1,0:T(8,128)(2,1)}, bf16[16,512,512]{2,1,0:T(8,128)(2,1)S(1)}, u32[]{:S(2)}) copy-start(bf16[16,512,512]{2,1,0:T(8,128)(2,1)S(1)} %select_convert_fusion.1) | copy-start | bytes 25165828
  94.0 3.4 %copy-start.6 = (f32[16,512,128]{1,2,0:T(8,128)S(1)}, f32[16,512,128]{1,2,0:T(8,128)}, u32[]{:S(2)}) copy-start(f32[16,512,128]{1,2,0:T(8,128)} %fusion.11) | copy-start | bytes 12582916
  97.4 2.6 copy-start.11
  132.4 5.6 %copy-start.12 = (f32[8192]{0:T(1024)S(1)}, f32[8192]{0:T(1024)}, u32[]{:S(2)}) copy-start(f32[8192]{0:T(1024)} %param.12) | copy-start | bytes 98308
  138.1 5.3 %copy-start.2 = (f32[128,8192]{1,0:T(8,128)S(1)}, f32[128,8192]{1,0:T(8,128)}, u32[]{:S(2)}) copy-start(f32[128,8192]{1,0:T(8,128)} %copy.81) | copy-start | bytes 12582916
  138.1 5.3 %copy-start.7 = (bf16[128,8192]{1,0:T(8,128)(2,1)S(1)}, bf16[128,8192]{1,0:T(8,128)(2,1)}, u32[]{:S(2)}) copy-start(bf16[128,8192]{1,0:T(8,128)(2,1)} %param.11) | copy-start | bytes 6291460
  138.1 5.9 %copy-start.8 = (bf16[128,8192]{1,0:T(8,128)(2,1)S(1)}, bf16[128,8192]{1,0:T(8,128)(2,1)}, u32[]{:S(2)}) copy-start(bf16[128,8192]{1,0:T(8,128)(2,1)} %param.13) | copy-start | bytes 6291460
  186.5 4.3 %copy-start.9 = (bf16[512,16,128]{0,2,1:T(8,128)(2,1)S(1)}, bf16[512,16,128]{0,2,1:T(8,128)(2,1)}, u32[]{:S(2)}) copy-start(bf16[512,16,128]{0,2,1:T(8,128)(2,1)} %copy.58) | copy-start | bytes 6291460
  190.7 4.9 %copy-start.3 = (bf16[16,512,512]{2,1,0:T(8,128)(2,1)}, bf16[16,512,512]{2,1,0:T(8,128)(2,1)S(1)}, u32[]{:S(2)}) copy-start(bf16[16,512,512]{2,1,0:T(8,128)(2,1)S(1)} %select_convert_fusion) | copy-start | bytes 25165828
  190.8 4.9 %copy-start.5 = (bf16[512,16,128]{0,2,1:T(8,128)(2,1)S(1)}, bf16[512,16,128]{0,2,1:T(8,128)(2,1)}, u32[]{:S(2)}) copy-start(bf16[512,16,128]{0,2,1:T(8,128)(2,1)} %copy.69) | copy-start | bytes 6291460
  270.2 3.4 %copy-start.4 = (f32[16,128,512]{2,1,0:T(8,128)S(1)}, f32[16,128,512]{2,1,0:T(8,128)}, u32[]{:S(2)}) copy-start(f32[16,128,512]{2,1,0:T(8,128)} %fusion.50) | copy-start | bytes 12582916
  270.2 4.4 %copy-start.10 = (bf16[512,2048]{1,0:T(8,128)(2,1)S(1)}, bf16[512,2048]{1,0:T(8,128)(2,1)}, u32[]{:S(2)}) copy-start(bf16[512,2048]{1,0:T(8,128)(2,1)} %param.9) | copy-start | bytes 6291460
Sparse Core Ops, SparseCore 0:
  18.4 75.5 all-gather.4
  186.6 70.4 all-gather.6
